TPU v7x, 512 devices: a whole 4x4x16 slice. The times are simulated.
512 devices in a mesh: prow: 32 (over y_hi, z), pcol: 16 (over y_lo, x, core).
Axes of the slice: x: 4, y: 4 (y_hi: 2, y_lo: 2; y = y_hi * 2 + y_lo), z: 16, core: 2. Of those that a mesh axis runs over, the one named last changes fastest.
Arguments:
- ainv: bfloat16 [3, 32, 256, 6, 16, 256], P(None, 'prow', None, None, 'pcol'), may hold values from -0.0390625 to 0.0390625
- panel: bfloat16 [6, 16, 256, 1536], P(None, 'pcol', None, 'prow'), may hold values from -6 to 6
- structure: int32 [4, 96], replicated, may hold values 0 or 1
- widths: int32 [4], replicated, may hold values from 1 to 512, 1536 in all
Outputs:
- inverse_panel: bfloat16 [3, 32, 256, 1536], P(None, 'prow', None, 'pcol')
Inputs may be any that keep to these rules, and one draw needn't show every extreme that they name: Supernode k owns the next widths[k] columns; the widths sum to 1536 and the widest is exactly 512.
All inputs are finite; a program needn't handle non-finite values.
Results may differ from a plain program's by a relative error of at most 0.001.
Values may be sent and summed in bfloat16 or wider, within the bound.
A program may use at most 64 MiB of HBM per device.

v0:
```python
import jax
import jax.numpy as jnp
from jax import lax
from jax.sharding import PartitionSpec as P


def column_onehot(widths, first, count, groups):
    ends = jnp.cumsum(widths, dtype=jnp.int32)
    columns = first + jnp.arange(count, dtype=jnp.int32)
    owner = jnp.sum((columns[:, None] >= ends[None, :]).astype(jnp.int32), axis=1)
    return (owner[:, None] == jnp.arange(groups, dtype=jnp.int32)[None, :]).astype(jnp.float32)


def body(ainv, panel, structure, widths):
    rows_here, _, blk, cols_here, _, _ = ainv.shape
    groups = structure.shape[0]
    nprow = lax.axis_size("prow")
    npcol = lax.axis_size("pcol")
    row_id = lax.axis_index("prow")
    col_id = lax.axis_index("pcol")
    width_in = panel.shape[3]
    total = width_in * nprow
    width_out = total // npcol
    struct_float = structure.astype(jnp.float32)
    panel_struct = lax.dynamic_slice_in_dim(
        struct_float.reshape(groups, cols_here, npcol), col_id, 1, 2
    )[:, :, 0]
    onehot_in = column_onehot(widths, row_id * width_in, width_in, groups)
    keep_in = jnp.dot(panel_struct.T, onehot_in.T)
    masked = panel[:, 0] * keep_in[:, None, :].astype(jnp.bfloat16)
    amat = ainv.reshape(rows_here * blk, cols_here * blk)
    piece = lax.all_gather(masked, "prow", axis=2, tiled=True)
    partial_prod = jnp.dot(
        amat, piece.reshape(cols_here * blk, piece.shape[2]), preferred_element_type=jnp.float32
    )
    summed = lax.psum_scatter(partial_prod, "pcol", scatter_dimension=1, tiled=True)
    out_struct = lax.dynamic_slice_in_dim(
        struct_float.reshape(groups, rows_here, nprow), row_id, 1, 2
    )[:, :, 0]
    onehot_out = column_onehot(widths, col_id * width_out, width_out, groups)
    keep_out = jnp.dot(out_struct.T, onehot_out.T)
    result = -(summed.reshape(rows_here, blk, width_out) * keep_out[:, None, :])
    return result.astype(jnp.bfloat16).reshape(rows_here, 1, blk, width_out)


def solution(mesh):
    in_specs = (P(None, "prow", None, None, "pcol", None), P(None, "pcol", None, "prow"), P(), P())
    out_specs = P(None, "prow", None, "pcol")
    return jax.shard_map(body, mesh=mesh, in_specs=in_specs, out_specs=out_specs, check_vma=False)
```

profile of v0, /device:TPU:32, one launch (start us, length us, event | category | flops | bytes accessed | tf_op | source)
XLA Modules:
  0.0 276.7 jit_solution(748920404496650673)
XLA Ops:
  6.5 0.0 all-gather.2.cloned.1.call-start
  6.5 0.7 convert_element_type.25
  7.2 0.1 reshape.69
  7.3 0.8 reduce-window.8
  8.1 0.2 dynamic-slice_reduce_fusion
  8.3 0.1 convert_reduce_fusion.1
  8.4 0.2 convolution_convert_fusion
  8.6 1.7 bitcast_multiply_fusion
  10.3 0.0 all-gather.2.cloned.1.call-update
  10.3 0.0 reduce-scatter.2.cloned.1.call-start
  10.3 3.1 %copy.21 = bf16[3,1,256,6,1,256]{5,3,2,0,4,1:T(8,128)(2,1)S(1)} copy(bf16[3,1,256,6,1,256]{5,2,4,3,1,0:T(8,128)(2,1)} %param.4) | data formatting | bytes 4718592 | tf_op args[0]
  13.4 0.8 copy.25
  14.2 168.6 %all-gather.2.cloned.1.call-done = bf16[6,256,1536]{1,2,0:T(8,128)(2,1)} async-done(((bf16[6,256,48]{1,2,0:T(8,128)(2,1)}), bf16[6,256,1536]{1,2,0:T(8,128)(2,1)}) %all-gather.2.cloned.1.call-update) | async-done | bytes 4718608 | tf_op jit(solution)/shard_map/all_gather | solution.py:32
  182.9 6.6 %copy.20 = bf16[6,256,1536]{2,1,0:T(8,128)(2,1)} copy(bf16[6,256,1536]{1,2,0:T(8,128)(2,1)} %all-gather.2.cloned.1.call-done) | data formatting | bytes 9437184 | tf_op jit(solution)/shard_map/all_gather | solution.py:32
  189.5 8.4 %convolution_bitcast_fusion = f32[768,1536]{0,1:T(8,128)} fusion(bf16[1536,1536]{1,0:T(8,128)(2,1)} %bitcast.18, bf16[768,1536]{1,0:T(8,128)(2,1)S(1)} %bitcast.19), kind=kOutput, calls=%fused_computation | convolution fusion | flops 3623878656 | bytes 11796480 | tf_op jit(solution)/shard_map/dot_general | solution.py:33
  197.9 0.0 reduce-scatter.2.cloned.1.call-update
  197.9 0.1 reshape.75
  198.0 0.2 dynamic-slice_reduce_fusion.1
  198.2 0.1 convert_reduce_fusion
  198.2 0.2 fusion
  198.4 69.5 %reduce-scatter.2.cloned.1.call-done = f32[768,96]{0,1:T(8,128)} async-done(((f32[768,1536]{0,1:T(8,128)}), f32[768,96]{0,1:T(8,128)}) %reduce-scatter.2.cloned.1.call-update) | async-done | bytes 294928 | tf_op jit(solution)/shard_map/reduce_scatter | solution.py:36
  267.9 1.1 reshape.74
  269.0 0.2 negate_convert_fusion
  269.2 0.7 copy.23
  (2 shorter events, 0.0 us)
Async XLA Ops:
  6.5 176.3 %all-gather.2.cloned.1.call-start = ((), (), s32[]{:S(2)}) async-start(), calls=%async_computation.1 | async-start | bytes 4866048 | tf_op jit(solution)/shard_map/all_gather | solution.py:32
  10.3 257.6 %reduce-scatter.2.cloned.1.call-start = ((), (), s32[]{:S(2)}) async-start(), calls=%async_computation.2 | async-start | bytes 5013504 | tf_op jit(solution)/shard_map/reduce_scatter | solution.py:36
Sparse Core Ops, SparseCore 0:
  10.5 172.3 all-gather.1
  198.0 69.8 reduce-scatter.1
where the time goes:
time: 277 us
  waiting for transfers between devices  238 us (86%)
  between operations  13.4 us (5%)
  local copies, waits for them, and re-layouts  12.8 us (5%)
  matrix products  8.8 us (3%)
  other arithmetic  3.55 us (1%)
    all_gather x1, waiting for transfers between devices, body(): piece = lax.all_gather(masked, 'prow', axis=2, tiled=True)  169 us
    reduce_scatter x1, waiting for transfers between devices, body(): lax.psum_scatter(partial_prod, 'pcol', scatter_dimension=1, tiled=True)  69.5 us
    dot_general x1, matrix products, body(): jnp.dot(amat, piece.reshape(cols_here * blk, piece.shape[2]), preferred_e...  8.4 us
    all_gather x1, local copies, waits for them, and re-layouts, body(): piece = lax.all_gather(masked, 'prow', axis=2, tiled=True)  6.62 us
  transfers between devices with their start and end apart: 2, of which 2 were waited for; matrix products, arithmetic and copies ran while one was open for 2% of the time, Pallas kernels for 0%

commit v1 on v0

v1 whole, which is shorter than its diff:
```python
import jax
import jax.numpy as jnp
from jax import lax
from jax.experimental import pallas as pl
from jax.experimental.pallas import tpu as pltpu
from jax.sharding import PartitionSpec as P

MESH = pl.DeviceIdType.MESH
NZ, NY, NX, NK = 16, 2, 4, 2


def column_keep(struct_ref, widths_ref, block, first, shape, axis):
    columns = first + lax.broadcasted_iota(jnp.int32, shape, axis)
    keep = jnp.zeros(shape, jnp.int32)
    low = jnp.int32(0)
    for k in range(struct_ref.shape[0]):
        high = low + widths_ref[k]
        inside = (columns >= low) & (columns < high)
        keep = keep + jnp.where(inside, struct_ref[k, block], 0)
        low = high
    return keep.astype(jnp.float32)


def kernel(struct_ref, widths_ref, p_ref, a_hbm, o_ref, abuf, pbuf, part, crecv, yrecv, xrecv, half,
           a_sem, pair_s, pair_r, up_s, up_r, dn_s, dn_r, core_s, core_r, y_s, y_r, x_s, x_r):
    row = lax.axis_index("prow")
    col = lax.axis_index("pcol")
    yh, z = row // NZ, row % NZ
    yl, x, k = col // (NX * NK), (col // NK) % NX, col % NK

    def dev(yh=yh, z=z, yl=yl, x=x, k=k):
        return (yh * NZ + z, (yl * NX + x) * NK + k)

    def z_at(step):
        return lax.rem(z + step + NZ, NZ)

    up_dev, dn_dev = dev(z=z_at(1)), dev(z=z_at(-1))
    pair_dev, core_dev, y_dev = dev(yh=1 - yh), dev(k=1 - k), dev(yl=1 - yl)
    x_devs = [dev(x=lax.rem(x + d, NX), k=kk) for d in range(1, NX) for kk in range(NK)]

    barrier = pltpu.get_barrier_semaphore()
    partners = [up_dev, dn_dev, pair_dev, core_dev, y_dev] + x_devs
    for d in partners:
        pl.semaphore_signal(barrier, inc=1, device_id=d, device_id_type=MESH)
    a_copy = pltpu.make_async_copy(a_hbm, abuf, a_sem)
    a_copy.start()
    blocks = p_ref.shape[0]
    npcol = lax.axis_size("pcol")
    for b in range(blocks):
        keep = column_keep(struct_ref, widths_ref, b * npcol + col, row * 48, (48, 256), 0)
        pbuf[z, yh, b] = (p_ref[b].astype(jnp.float32) * keep).astype(jnp.bfloat16)
    pl.semaphore_wait(barrier, len(partners))

    def remote(src, dst, send, recv, device):
        return pltpu.make_async_remote_copy(
            src_ref=src, dst_ref=dst, send_sem=send, recv_sem=recv, device_id=device, device_id_type=MESH)

    def pair():
        return remote(pbuf.at[z, yh], pbuf.at[z, yh], pair_s, pair_r, pair_dev)

    def pair_in():
        return remote(pbuf.at[z, 1 - yh], pbuf.at[z, 1 - yh], pair_s, pair_r, pair_dev)

    def up(s, q, zz):
        y = yh if q == 0 else 1 - yh
        return remote(pbuf.at[zz, y], pbuf.at[zz, y], up_s.at[s, q], up_r.at[s, q], up_dev)

    def dn(s, q, zz):
        y = yh if q == 0 else 1 - yh
        return remote(pbuf.at[zz, y], pbuf.at[zz, y], dn_s.at[s, q], dn_r.at[s, q], dn_dev)

    def products(zs):
        n = len(zs)
        for a in range(abuf.shape[0]):
            total = None
            for b in range(blocks):
                rows = [pbuf[zz, :, b].reshape(96, 256) for zz in zs]
                lhs = rows[0] if n == 1 else jnp.concatenate(rows, axis=0)
                term = lax.dot_general(lhs, abuf[a, b], (((1,), (1,)), ((), ())), preferred_element_type=jnp.float32)
                total = term if total is None else total + term
            for i, zz in enumerate(zs):
                piece = total[96 * i:96 * i + 96].reshape(2, 48, 256)
                if a == 0:
                    part[zz, 0, :, :, 0:256] = piece
                elif a == 1:
                    part[zz, 0, :, :, 256:384] = piece[:, :, 0:128]
                    part[zz, 1, :, :, 0:128] = piece[:, :, 128:256]
                else:
                    part[zz, 1, :, :, 128:384] = piece

    def core(t, zz):
        return remote(part.at[zz, 1 - k], crecv.at[zz], core_s.at[t], core_r.at[t], core_dev)

    def ycopy(t, zz):
        return remote(part.at[zz, k, 1 - yl], yrecv.at[zz], y_s.at[t], y_r.at[t], y_dev)

    def xcopy(t, zz):
        xo, ko, h = zz // 4, (zz // 2) % 2, zz % 2
        slot = lax.rem(x - xo + NX, NX) * NK + lax.rem(k - ko + NK, NK)
        return remote(part.at[zz, k, yl], xrecv.at[slot, h], x_s.at[t], x_r.at[slot, h], dev(x=xo, k=ko))

    def mine(zz):
        return zz // 2 == x * 2 + k

    def stage_core(t, zz):
        core(t, zz).start()

    def stage_y(t, zz):
        core(t, zz).wait_recv()
        part[zz, k] = part[zz, k] + crecv[zz]
        ycopy(t, zz).start()

    def stage_x(t, zz):
        ycopy(t, zz).wait_recv()
        part[zz, k, yl] = part[zz, k, yl] + yrecv[zz]

        @pl.when(jnp.logical_not(mine(zz)))
        def _():
            xcopy(t, zz).start()

    def at(s):
        if isinstance(s, int) and s == 0:
            return [(0, z)]
        if isinstance(s, int) and s == 8:
            return [(15, z_at(8))]
        return [(2 * s - 1, z_at(-s)), (2 * s, z_at(s))]

    def step(s):
        last, fwd = isinstance(s, int) and s == 8, not (isinstance(s, int) and s >= 7)
        for q in range(2):
            if not (last and q == 1):
                up(s, q, z_at(-s)).wait_recv()
                if fwd or (not last and q == 0):
                    up(s + 1, q, z_at(-s)).start()
            if not (last and q == 0):
                dn(s, q, z_at(s)).wait_recv()
                if fwd or (not last and q == 1):
                    dn(s + 1, q, z_at(s)).start()
            if q == 0:
                for t, zz in at(s - 1):
                    stage_y(t, zz)
        products([zz for _, zz in at(s)])
        for t, zz in at(s):
            stage_core(t, zz)
        if not (isinstance(s, int) and s < 2):
            for t, zz in at(s - 2 if not isinstance(s, int) else s - 2):
                stage_x(t, zz)

    pair().start()
    up(1, 0, z).start()
    dn(1, 0, z).start()
    a_copy.wait()
    pair_in().wait_recv()
    up(1, 1, z).start()
    dn(1, 1, z).start()
    products([z])
    stage_core(0, z)
    step(1)
    step(2)

    @pl.loop(3, 7)
    def _(s):
        step(s)

    step(7)
    step(8)
    for t, zz in at(7):
        stage_x(t, zz)
    for t, zz in at(8):
        stage_y(t, zz)
    for t, zz in at(8):
        stage_x(t, zz)

    for h in range(2):
        zz = 4 * x + 2 * k + h
        for slot in range(1, 8):
            remote(xrecv.at[slot, h], xrecv.at[slot, h], x_s.at[0], x_r.at[slot, h], core_dev).wait_recv()
        half[k] = part[zz, k, yl] + xrecv[2, h] + xrecv[4, h] + xrecv[6, h]
        half[1 - k] = xrecv[1, h] + xrecv[3, h] + xrecv[5, h] + xrecv[7, h]
        nprow = lax.axis_size("prow")
        lanes = [half[0, :, 0:256], jnp.concatenate([half[0, :, 256:384], half[1, :, 0:128]], axis=1), half[1, :, 128:384]]
        for a in range(3):
            keep = column_keep(struct_ref, widths_ref, a * nprow + row, col * 96 + 48 * h, (48, 256), 0)
            o_ref[a, 48 * h:48 * h + 48, :] = (-(lanes[a] * keep)).astype(jnp.bfloat16)

    pair().wait_send()
    for s in range(1, 9):
        for q in range(2):
            if s < 8 or q == 0:
                up(s, q, z).wait_send()
            if s < 8 or q == 1:
                dn(s, q, z).wait_send()
    for s in range(9):
        for t, zz in at(s):
            core(t, zz).wait_send()
            ycopy(t, zz).wait_send()

            @pl.when(jnp.logical_not(mine(zz)))
            def _(t=t, zz=zz):
                xcopy(t, zz).wait_send()


def body(ainv, panel, structure, widths):
    a = ainv[:, 0, :, :, 0, :].transpose(0, 2, 1, 3)
    p = panel[:, 0].transpose(0, 2, 1)
    dma = pltpu.SemaphoreType.DMA
    f32, bf16 = jnp.float32, jnp.bfloat16
    out = pl.pallas_call(
        kernel,
        out_shape=jax.ShapeDtypeStruct((3, 96, 256), bf16),
        in_specs=[pl.BlockSpec(memory_space=pltpu.SMEM), pl.BlockSpec(memory_space=pltpu.SMEM),
                  pl.BlockSpec(memory_space=pltpu.VMEM), pl.BlockSpec(memory_space=pl.ANY)],
        out_specs=pl.BlockSpec(memory_space=pltpu.VMEM),
        scratch_shapes=[
            pltpu.VMEM((3, 6, 256, 256), bf16),
            pltpu.VMEM((NZ, NY, 6, 48, 256), bf16),
            pltpu.VMEM((NZ, 2, 2, 48, 384), f32),
            pltpu.VMEM((NZ, 2, 48, 384), f32),
            pltpu.VMEM((NZ, 48, 384), f32),
            pltpu.VMEM((8, 2, 48, 384), f32),
            pltpu.VMEM((2, 48, 384), f32),
            dma, dma, dma, dma((9, 2)), dma((9, 2)), dma((9, 2)), dma((9, 2)),
            dma((16,)), dma((16,)), dma((16,)), dma((16,)), dma((16,)), dma((8, 2)),
        ],
        compiler_params=pltpu.CompilerParams(
            collective_id=0, has_side_effects=True, vmem_limit_bytes=48 << 20),
        name="gather_multiply_scatter",
    )(structure, widths, p, a)
    return out.transpose(0, 2, 1)[:, None]


def solution(mesh):
    in_specs = (P(None, "prow", None, None, "pcol", None), P(None, "pcol", None, "prow"), P(), P())
    out_specs = P(None, "prow", None, "pcol")
    return jax.shard_map(body, mesh=mesh, in_specs=in_specs, out_specs=out_specs, check_vma=False)
```

time: 277 us -> 85.4 us (0.31)
  the two profiles are of different devices: /device:TPU:32 before, /device:TPU:36 now
where the time goes in v1:
time: 85.4 us; the launch traced here: 85.2 us
  Pallas kernels  80.6 us (94%)
  local copies, waits for them, and re-layouts  4.57 us (5%)
    pallas_call x1, Pallas kernels, body(): pl.pallas_call(kernel, out_shape=jax.ShapeDtypeStruct((3, 96, 256), bf16)...  80.6 us
    unnamed x9, local copies, waits for them, and re-layouts  4.57 us

profile of v1, /device:TPU:36, one launch (start us, length us, event | category | flops | bytes accessed | tf_op | source)
XLA Modules:
  0.0 85.2 jit_solution(9592664720389368847)
XLA Ops:
  0.0 0.0 copy-start
  0.0 1.7 %copy-done = bf16[3,1,256,6,1,256]{5,2,4,3,1,0:T(8,128)(2,1)S(1)} copy-done((bf16[3,1,256,6,1,256]{5,2,4,3,1,0:T(8,128)(2,1)S(1)}, bf16[3,1,256,6,1,256]{5,2,4,3,1,0:T(8,128)(2,1)}, u32[]{:S(2)}) %copy-start) | copy-done | bytes 2359320
  1.7 0.0 copy-start.1
  1.7 0.9 %copy-done.1 = bf16[6,1,256,48]{2,3,1,0:T(8,128)(2,1)S(1)} copy-done((bf16[6,1,256,48]{2,3,1,0:T(8,128)(2,1)S(1)}, bf16[6,1,256,48]{2,3,1,0:T(8,128)(2,1)}, u32[]{:S(2)}) %copy-start.1) | copy-done | bytes 147480
  2.6 0.0 copy-start.2
  2.6 0.7 copy-done.2
  3.3 0.0 copy-start.3
  3.3 0.7 copy-done.3
  3.9 80.6 %gather_multiply_scatter.1 = bf16[3,96,256]{2,1,0:T(8,128)(2,1)S(1)} custom-call(s32[4,96]{1,0:T(4,128)S(1)} %copy-done.2, s32[4]{0:T(128)S(1)} %copy-done.3, bf16[6,48,256]{2,1,0:T(8,128)(2,1)S(1)} %bitcast.13, bf16[3,6,256,256]{3,2,1,0:T(8,128)(2,1)S(1)} %bitcast.11), custom_call_target="tpu_custom_call" | custom-call | tf_op jit(solution)/shard_map/gather_multiply_scatter/pallas_call | solution.py:208
  84.5 0.7 copy.7
Async XLA Ops:
  0.0 1.7 %copy-start = (bf16[3,1,256,6,1,256]{5,2,4,3,1,0:T(8,128)(2,1)S(1)}, bf16[3,1,256,6,1,256]{5,2,4,3,1,0:T(8,128)(2,1)}, u32[]{:S(2)}) copy-start(bf16[3,1,256,6,1,256]{5,2,4,3,1,0:T(8,128)(2,1)} %param.4) | copy-start | bytes 7077892
  1.7 0.9 %copy-start.1 = (bf16[6,1,256,48]{2,3,1,0:T(8,128)(2,1)S(1)}, bf16[6,1,256,48]{2,3,1,0:T(8,128)(2,1)}, u32[]{:S(2)}) copy-start(bf16[6,1,256,48]{2,3,1,0:T(8,128)(2,1)} %param.5) | copy-start | bytes 442372
  2.6 0.7 copy-start.2
  3.3 0.7 copy-start.3

commit v2 on v0

v2 whole, which is shorter than its diff:
```python
import jax
import jax.numpy as jnp
from jax import lax
from jax.experimental import pallas as pl
from jax.experimental.pallas import tpu as pltpu
from jax.sharding import PartitionSpec as P

MESH = pl.DeviceIdType.MESH
NZ, NY, NX, NK = 16, 2, 4, 2


def supernode_masks(widths_ref, first, shape):
    columns = first + lax.broadcasted_iota(jnp.int32, shape, 0)
    masks, low = [], jnp.int32(0)
    for k in range(widths_ref.shape[0]):
        high = low + widths_ref[k]
        masks.append((columns >= low) & (columns < high))
        low = high
    return masks


def keep_of(masks, struct_ref, block):
    keep = jnp.zeros(masks[0].shape, jnp.int32)
    for k, mask in enumerate(masks):
        keep = keep + jnp.where(mask, struct_ref[k, block], 0)
    return keep.astype(jnp.float32)


def kernel(struct_hbm, widths_hbm, p_hbm, a_hbm, o_ref, struct_ref, widths_ref, own, abuf, pbuf, part, crecv, xrecv, yrecv,
           frecv, half, in_sem, pair_s, pair_r, up_s, up_r, dn_s, dn_r, late_s, late_r, core_s, core_r, x_s, x_r, y_s, y_r,
           f_s, f_r):
    row = lax.axis_index("prow")
    col = lax.axis_index("pcol")
    nprow, npcol = lax.axis_size("prow"), lax.axis_size("pcol")
    yh, z = row // NZ, row % NZ
    yl, x, k = col // (NX * NK), (col // NK) % NX, col % NK

    def dev(yh=yh, z=z, yl=yl, x=x, k=k):
        return (yh * NZ + z, (yl * NX + x) * NK + k)

    def z_at(step):
        return lax.rem(z + step + NZ, NZ)

    loads = [pltpu.make_async_copy(src, dst, in_sem.at[i]) for i, (src, dst) in enumerate(
        [(struct_hbm, struct_ref), (widths_hbm, widths_ref), (p_hbm, own), (a_hbm, abuf)])]
    for load in loads:
        load.start()
    up_dev, dn_dev = dev(z=z_at(1)), dev(z=z_at(-1))
    pair_dev, core_dev, y_dev = dev(yh=1 - yh), dev(k=1 - k), dev(yl=1 - yl)
    partners = [up_dev, dn_dev, pair_dev, core_dev, y_dev] + [dev(x=lax.rem(x + d, NX)) for d in range(1, NX)]
    barrier = pltpu.get_barrier_semaphore()
    for d in partners:
        pl.semaphore_signal(barrier, inc=1, device_id=d, device_id_type=MESH)
    for load in loads[:3]:
        load.wait()
    masks = supernode_masks(widths_ref, row * 48, (48, 256))
    for b in range(6):
        keep = keep_of(masks, struct_ref, b * npcol + col)
        pbuf[z, yh, b] = (own[b].astype(jnp.float32) * keep).astype(jnp.bfloat16)
    pl.semaphore_wait(barrier, len(partners))

    def remote(src, dst, send, recv, device):
        return pltpu.make_async_remote_copy(
            src_ref=src, dst_ref=dst, send_sem=send, recv_sem=recv, device_id=device, device_id_type=MESH)

    def piece(zz, y, second):
        return pbuf.at[zz, y, pl.ds(3 if second else 0, 3)]

    def ring(sems, device):
        def message(s, h, zz):
            ref = piece(zz, 1 - yh if h == 2 else yh, h == 1)
            return remote(ref, ref, sems[0].at[s, h], sems[1].at[s, h], device)
        return message

    up, dn = ring((up_s, up_r), up_dev), ring((dn_s, dn_r), dn_dev)

    def pair(y):
        return remote(piece(z, y, False), piece(z, y, False), pair_s, pair_r, pair_dev)

    def late(t, zz, y):
        return remote(piece(zz, y, True), piece(zz, y, True), late_s.at[t], late_r.at[t], pair_dev)

    def products(zs):
        n = len(zs)
        for a in range(3):
            total = None
            for b in range(6):
                rows = [pbuf[zz, :, b].reshape(96, 256) for zz in zs]
                lhs = rows[0] if n == 1 else jnp.concatenate(rows, axis=0)
                term = lax.dot_general(lhs, abuf[a, b], (((1,), (1,)), ((), ())), preferred_element_type=jnp.float32)
                total = term if total is None else total + term
            for i, zz in enumerate(zs):
                got = total[96 * i:96 * i + 96].reshape(2, 48, 256)
                if a == 0:
                    part[zz, 0, :, :, 0:256] = got
                elif a == 1:
                    part[zz, 0, :, :, 256:384] = got[:, :, 0:128]
                    part[zz, 1, :, :, 0:128] = got[:, :, 128:256]
                else:
                    part[zz, 1, :, :, 128:384] = got

    def core(t, zz):
        return remote(part.at[zz, 1 - k], crecv.at[zz], core_s.at[t], core_r.at[t], core_dev)

    def xcopy(t, zz):
        slot = lax.rem(x - zz // 4 + NX, NX) - 1
        return remote(part.at[zz, k], xrecv.at[slot, zz % 4], x_s.at[t], x_r.at[slot, zz % 4], dev(x=zz // 4))

    def xcopy_in(slot, zz):
        return remote(part.at[zz, k], xrecv.at[slot, zz % 4], x_s.at[0], x_r.at[slot, zz % 4], core_dev)

    def ycopy(zz):
        return remote(part.at[zz, k, 1 - yl], yrecv.at[zz % 4], y_s.at[zz % 4], y_r.at[zz % 4], y_dev)

    def fcopy(zz):
        return remote(part.at[zz, k, yl], frecv.at[zz % 2], f_s.at[zz % 2], f_r.at[zz % 2], core_dev)

    def stage_x(t, zz):
        core(t, zz).wait_recv()
        part[zz, k] = part[zz, k] + crecv[zz]

        @pl.when(zz // 4 != x)
        def _():
            xcopy(t, zz).start()

    def stage_y(t, zz):
        @pl.when(zz // 4 == x)
        def _():
            for slot in range(3):
                xcopy_in(slot, zz).wait_recv()
            j = zz % 4
            part[zz, k] = part[zz, k] + xrecv[0, j] + xrecv[1, j] + xrecv[2, j]
            ycopy(zz).start()

    def stage_f(t, zz):
        @pl.when(zz // 4 == x)
        def _():
            ycopy(zz).wait_recv()
            part[zz, k, yl] = part[zz, k, yl] + yrecv[zz % 4]

            @pl.when((zz // 2) % 2 != k)
            def _():
                fcopy(zz).start()

    def items(s):
        if isinstance(s, int):
            if s == 0:
                return [(0, z)]
            if s == 8:
                return [(15, z_at(8))]
        return [(2 * s - 1, z_at(-s)), (2 * s, z_at(s))]

    def run(stage, s):
        if isinstance(s, int):
            for t, zz in items(s) if s >= 0 else []:
                stage(t, zz)
            return
        for t, zz in items(s):
            @pl.when(t >= 0)
            def _(t=t, zz=zz):
                stage(t, lax.rem(zz + NZ, NZ))

    def multiply(s):
        for t, zz in items(s):
            late(t, zz, 1 - yh).wait_recv()
        products([zz for _, zz in items(s)])
        for t, zz in items(s):
            core(t, zz).start()

    def when(s, do):
        if isinstance(s, int):
            if s < 7:
                do()
        else:
            pl.when(s < 7)(do)

    def step(s):
        last = isinstance(s, int) and s == 8
        below, above = z_at(-s), z_at(s)
        up(s, 0, below).wait_recv()
        if not last:
            up(s + 1, 0, below).start()
            dn(s, 0, above).wait_recv()
            when(s, dn(s + 1, 0, above).start)
        multiply(s - 1)
        if not last:
            up(s, 1, below).wait_recv()
            when(s, up(s + 1, 1, below).start)
        dn(s, 1, above).wait_recv()
        if not last:
            dn(s + 1, 1, above).start()
        for t, zz in items(s):
            late(t, zz, yh).start()
        run(stage_x, s - 2)
        up(s, 2, below).wait_recv()
        if not last:
            up(s + 1, 2, below).start()
            dn(s, 2, above).wait_recv()
            when(s, dn(s + 1, 2, above).start)
        run(stage_y, s - 4)
        run(stage_f, s - 5)

    for h in range(2):
        up(1, h, z).start()
        dn(1, h, z).start()
        if h == 0:
            pair(yh).start()
    late(0, z, yh).start()
    loads[3].wait()
    pair(1 - yh).wait_recv()
    up(1, 2, z).start()
    dn(1, 2, z).start()
    step(1)

    @pl.loop(2, 8)
    def _(s):
        step(s)

    step(8)
    multiply(8)
    run(stage_x, 7)
    run(stage_y, 5)
    run(stage_f, 4)
    run(stage_x, 8)
    run(stage_y, 6)
    run(stage_f, 5)
    run(stage_y, 7)
    run(stage_f, 6)
    run(stage_y, 8)
    run(stage_f, 7)
    run(stage_f, 8)

    masks = supernode_masks(widths_ref, col * 96, (96, 256))
    keeps = [keep_of(masks, struct_ref, a * nprow + row) for a in range(3)]
    for h in range(2):
        zz = 4 * x + 2 * k + h
        fcopy(zz).wait_recv()
        half[k] = part[zz, k, yl]
        half[1 - k] = frecv[h]
        lanes = [half[0, :, 0:256], jnp.concatenate([half[0, :, 256:384], half[1, :, 0:128]], axis=1), half[1, :, 128:384]]
        for a in range(3):
            o_ref[a, 48 * h:48 * h + 48, :] = (-(lanes[a] * keeps[a][48 * h:48 * h + 48])).astype(jnp.bfloat16)

    pair(yh).wait_send()

    @pl.loop(1, 8)
    def _(s):
        for h in range(3):
            up(s, h, z).wait_send()
            dn(s, h, z).wait_send()

    up(8, 0, z).wait_send()
    up(8, 2, z).wait_send()
    dn(8, 1, z).wait_send()

    @pl.loop(0, 16)
    def _(t):
        s = (t + 1) // 2
        zz = lax.rem(z + jnp.where(t % 2 == 1, -s, s) + NZ, NZ)
        late(t, zz, yh).wait_send()
        core(t, zz).wait_send()

        @pl.when(zz // 4 != x)
        def _():
            xcopy(t, zz).wait_send()

    for j in range(4):
        ycopy(4 * x + j).wait_send()
    for h in range(2):
        fcopy(4 * x + 2 * (1 - k) + h).wait_send()


def body(ainv, panel, structure, widths):
    a = ainv[:, 0, :, :, 0, :].transpose(0, 2, 1, 3)
    p = panel[:, 0].transpose(0, 2, 1)
    dma, vmem = pltpu.SemaphoreType.DMA, pltpu.VMEM
    f32, bf16 = jnp.float32, jnp.bfloat16
    out = pl.pallas_call(
        kernel,
        out_shape=jax.ShapeDtypeStruct((3, 96, 256), bf16),
        in_specs=[pl.BlockSpec(memory_space=pl.ANY)] * 4,
        out_specs=pl.BlockSpec(memory_space=vmem),
        scratch_shapes=[
            pltpu.SMEM((4, 96), jnp.int32), pltpu.SMEM((4,), jnp.int32), vmem((6, 48, 256), bf16),
            vmem((3, 6, 256, 256), bf16),
            vmem((NZ, NY, 6, 48, 256), bf16),
            vmem((NZ, 2, 2, 48, 384), f32),
            vmem((NZ, 2, 48, 384), f32),
            vmem((3, 4, 2, 48, 384), f32),
            vmem((4, 48, 384), f32),
            vmem((2, 48, 384), f32),
            vmem((2, 48, 384), f32),
            dma((4,)), dma, dma, dma((9, 3)), dma((9, 3)), dma((9, 3)), dma((9, 3)),
            dma((16,)), dma((16,)), dma((16,)), dma((16,)), dma((16,)), dma((3, 4)),
            dma((4,)), dma((4,)), dma((2,)), dma((2,)),
        ],
        compiler_params=pltpu.CompilerParams(
            collective_id=0, has_side_effects=True, vmem_limit_bytes=60 << 20),
        name="gather_multiply_scatter",
    )(structure, widths, p, a)
    return out.transpose(0, 2, 1)[:, None]


def solution(mesh):
    in_specs = (P(None, "prow", None, None, "pcol", None), P(None, "pcol", None, "prow"), P(), P())
    out_specs = P(None, "prow", None, "pcol")
    return jax.shard_map(body, mesh=mesh, in_specs=in_specs, out_specs=out_specs, check_vma=False)
```

time: 277 us -> 94.7 us (0.34)
  the two profiles are of different devices: /device:TPU:32 before, /device:TPU:36 now
where the time goes in v2:
time: 94.7 us; the launch traced here: 94.5 us
  Pallas kernels  92.9 us (98%)
  local copies, waits for them, and re-layouts  1.58 us (2%)
    pallas_call x1, Pallas kernels, body(): pl.pallas_call(kernel, out_shape=jax.ShapeDtypeStruct((3, 96, 256), bf16)...  92.9 us

profile of v2, /device:TPU:36, one launch (start us, length us, event | category | flops | bytes accessed | tf_op | source)
XLA Modules:
  0.0 94.5 jit_solution(5261379293178629317)
XLA Ops:
  0.0 92.9 %gather_multiply_scatter.1 = bf16[3,96,256]{2,1,0:T(8,128)(2,1)} custom-call(s32[4,96]{1,0:T(4,128)} %struct_hbm.1, s32[4]{0:T(128)} %widths_hbm.1, bf16[6,48,256]{2,1,0:T(8,128)(2,1)} %bitcast.13, bf16[3,6,256,256]{3,2,1,0:T(8,128)(2,1)} %bitcast.11), custom_call_target="tpu_custom_call" | custom-call | tf_op jit(solution)/shard_map/gather_multiply_scatter/pallas_call | solution.py:278
  93.0 1.6 %copy.7 = bf16[3,1,256,96]{2,3,1,0:T(8,128)(2,1)} copy(bf16[3,1,256,96]{2,3,1,0:T(8,128)(2,1)} %bitcast.12) | data formatting | bytes 294912

commit v3 on v2

--- a/solution.py
+++ b/solution.py
@@ -26,9 +26,8 @@
     return keep.astype(jnp.float32)
 
 
-def kernel(struct_hbm, widths_hbm, p_hbm, a_hbm, o_ref, struct_ref, widths_ref, own, abuf, pbuf, part, crecv, xrecv, yrecv,
-           frecv, half, in_sem, pair_s, pair_r, up_s, up_r, dn_s, dn_r, late_s, late_r, core_s, core_r, x_s, x_r, y_s, y_r,
-           f_s, f_r):
+def kernel(struct_hbm, widths_hbm, p_hbm, a_hbm, o_ref, struct_ref, widths_ref, own, abuf, pbuf, part, crecv, xrecv, frecv,
+           in_sem, pair_s, pair_r, up_s, up_r, dn_s, dn_r, late_s, late_r, core_s, core_r, x_s, x_r, f_s, f_r):
     row = lax.axis_index("prow")
     col = lax.axis_index("pcol")
     nprow, npcol = lax.axis_size("prow"), lax.axis_size("pcol")
@@ -46,8 +45,8 @@
     for load in loads:
         load.start()
     up_dev, dn_dev = dev(z=z_at(1)), dev(z=z_at(-1))
-    pair_dev, core_dev, y_dev = dev(yh=1 - yh), dev(k=1 - k), dev(yl=1 - yl)
-    partners = [up_dev, dn_dev, pair_dev, core_dev, y_dev] + [dev(x=lax.rem(x + d, NX)) for d in range(1, NX)]
+    pair_dev, core_dev = dev(yh=1 - yh), dev(k=1 - k)
+    partners = [up_dev, dn_dev, pair_dev] + [(row, lax.rem(col + d, npcol)) for d in range(1, npcol)]
     barrier = pltpu.get_barrier_semaphore()
     for d in partners:
         pl.semaphore_signal(barrier, inc=1, device_id=d, device_id_type=MESH)
@@ -68,17 +67,17 @@
 
     def ring(sems, device):
         def message(s, h, zz):
-            ref = piece(zz, 1 - yh if h == 2 else yh, h == 1)
+            ref = piece(zz, 1 - yh if h == 2 else yh, h > 0)
             return remote(ref, ref, sems[0].at[s, h], sems[1].at[s, h], device)
         return message
 
     up, dn = ring((up_s, up_r), up_dev), ring((dn_s, dn_r), dn_dev)
 
     def pair(y):
-        return remote(piece(z, y, False), piece(z, y, False), pair_s, pair_r, pair_dev)
+        return remote(piece(z, y, True), piece(z, y, True), pair_s, pair_r, pair_dev)
 
     def late(t, zz, y):
-        return remote(piece(zz, y, True), piece(zz, y, True), late_s.at[t], late_r.at[t], pair_dev)
+        return remote(piece(zz, y, False), piece(zz, y, False), late_s.at[t], late_r.at[t], pair_dev)
 
     def products(zs):
         n = len(zs)
@@ -90,7 +89,7 @@
                 term = lax.dot_general(lhs, abuf[a, b], (((1,), (1,)), ((), ())), preferred_element_type=jnp.float32)
                 total = term if total is None else total + term
             for i, zz in enumerate(zs):
-                got = total[96 * i:96 * i + 96].reshape(2, 48, 256)
+                got = total[96 * i:96 * i + 96].reshape(4, 24, 256)
                 if a == 0:
                     part[zz, 0, :, :, 0:256] = got
                 elif a == 1:
@@ -102,45 +101,36 @@
     def core(t, zz):
         return remote(part.at[zz, 1 - k], crecv.at[zz], core_s.at[t], core_r.at[t], core_dev)
 
-    def xcopy(t, zz):
-        slot = lax.rem(x - zz // 4 + NX, NX) - 1
-        return remote(part.at[zz, k], xrecv.at[slot, zz % 4], x_s.at[t], x_r.at[slot, zz % 4], dev(x=zz // 4))
-
-    def xcopy_in(slot, zz):
-        return remote(part.at[zz, k], xrecv.at[slot, zz % 4], x_s.at[0], x_r.at[slot, zz % 4], core_dev)
-
-    def ycopy(zz):
-        return remote(part.at[zz, k, 1 - yl], yrecv.at[zz % 4], y_s.at[zz % 4], y_r.at[zz % 4], y_dev)
-
-    def fcopy(zz):
-        return remote(part.at[zz, k, yl], frecv.at[zz % 2], f_s.at[zz % 2], f_r.at[zz % 2], core_dev)
-
-    def stage_x(t, zz):
+    def xcopy(t, zz, d):
+        to = lax.rem(x + d, NX)
+        return remote(part.at[zz, k, to], xrecv.at[zz, d - 1], x_s.at[t, d - 1], x_r.at[t, d - 1], dev(x=to))
+
+    def owned_here(zz):
+        return (zz // 4 == x) & (x // 2 == yl) & ((zz // 2) % 2 == k)
+
+    def fcopy(t, zz):
+        h, rh = zz % 2, x % 2
+        return remote(part.at[zz, k, x], frecv.at[h, rh, yl, k], f_s.at[t], f_r.at[h, rh, yl, k],
+                      dev(x=zz // 4, yl=x // 2, k=(zz // 2) % 2))
+
+    def stage_c(t, zz):
         core(t, zz).wait_recv()
         part[zz, k] = part[zz, k] + crecv[zz]
-
-        @pl.when(zz // 4 != x)
+        for d in (2, 1, 3):
+            xcopy(t, zz, d).start()
+
+    def stage_s(t, zz):
+        for d in (2, 1, 3):
+            xcopy(t, zz, d).wait_recv()
+        part[zz, k, x] = part[zz, k, x] + xrecv[zz, 0] + xrecv[zz, 1] + xrecv[zz, 2]
+
+        @pl.when(owned_here(zz))
         def _():
-            xcopy(t, zz).start()
-
-    def stage_y(t, zz):
-        @pl.when(zz // 4 == x)
+            frecv[zz % 2, x % 2, yl, k] = part[zz, k, x]
+
+        @pl.when(jnp.logical_not(owned_here(zz)))
         def _():
-            for slot in range(3):
-                xcopy_in(slot, zz).wait_recv()
-            j = zz % 4
-            part[zz, k] = part[zz, k] + xrecv[0, j] + xrecv[1, j] + xrecv[2, j]
-            ycopy(zz).start()
-
-    def stage_f(t, zz):
-        @pl.when(zz // 4 == x)
-        def _():
-            ycopy(zz).wait_recv()
-            part[zz, k, yl] = part[zz, k, yl] + yrecv[zz % 4]
-
-            @pl.when((zz // 2) % 2 != k)
-            def _():
-                fcopy(zz).start()
+            fcopy(t, zz).start()
 
     def items(s):
         if isinstance(s, int):
@@ -182,23 +172,23 @@
             up(s + 1, 0, below).start()
             dn(s, 0, above).wait_recv()
             when(s, dn(s + 1, 0, above).start)
-        multiply(s - 1)
+        for t, zz in items(s):
+            late(t, zz, yh).start()
+        if not (isinstance(s, int) and s < 2):
+            multiply(s - 2)
         if not last:
             up(s, 1, below).wait_recv()
             when(s, up(s + 1, 1, below).start)
         dn(s, 1, above).wait_recv()
         if not last:
             dn(s + 1, 1, above).start()
-        for t, zz in items(s):
-            late(t, zz, yh).start()
-        run(stage_x, s - 2)
+        run(stage_c, s - 3)
         up(s, 2, below).wait_recv()
         if not last:
             up(s + 1, 2, below).start()
             dn(s, 2, above).wait_recv()
             when(s, dn(s + 1, 2, above).start)
-        run(stage_y, s - 4)
-        run(stage_f, s - 5)
+        run(stage_s, s - 5)
 
     for h in range(2):
         up(1, h, z).start()
@@ -211,33 +201,41 @@
     up(1, 2, z).start()
     dn(1, 2, z).start()
     step(1)
-
-    @pl.loop(2, 8)
+    step(2)
+
+    @pl.loop(3, 8)
     def _(s):
         step(s)
 
     step(8)
+    multiply(7)
+    run(stage_c, 6)
+    run(stage_s, 4)
     multiply(8)
-    run(stage_x, 7)
-    run(stage_y, 5)
-    run(stage_f, 4)
-    run(stage_x, 8)
-    run(stage_y, 6)
-    run(stage_f, 5)
-    run(stage_y, 7)
-    run(stage_f, 6)
-    run(stage_y, 8)
-    run(stage_f, 7)
-    run(stage_f, 8)
+    run(stage_c, 7)
+    run(stage_s, 5)
+    run(stage_c, 8)
+    run(stage_s, 6)
+    run(stage_s, 7)
+    run(stage_s, 8)
 
     masks = supernode_masks(widths_ref, col * 96, (96, 256))
     keeps = [keep_of(masks, struct_ref, a * nprow + row) for a in range(3)]
     for h in range(2):
         zz = 4 * x + 2 * k + h
-        fcopy(zz).wait_recv()
-        half[k] = part[zz, k, yl]
-        half[1 - k] = frecv[h]
-        lanes = [half[0, :, 0:256], jnp.concatenate([half[0, :, 256:384], half[1, :, 0:128]], axis=1), half[1, :, 128:384]]
+        halves = []
+        for rh in range(2):
+            for ys in range(2):
+                for ks in range(2):
+                    here = (x == 2 * yl + rh) & (ys == yl) & (ks == k)
+
+                    @pl.when(jnp.logical_not(here))
+                    def _(rh=rh, ys=ys, ks=ks):
+                        remote(frecv.at[h, rh, ys, ks], frecv.at[h, rh, ys, ks], f_s.at[0], f_r.at[h, rh, ys, ks],
+                               core_dev).wait_recv()
+        halves = [jnp.concatenate([frecv[h, rh, 0, ks] + frecv[h, rh, 1, ks] for rh in range(2)], axis=0) for ks in range(2)]
+        lanes = [halves[0][:, 0:256], jnp.concatenate([halves[0][:, 256:384], halves[1][:, 0:128]], axis=1),
+                 halves[1][:, 128:384]]
         for a in range(3):
             o_ref[a, 48 * h:48 * h + 48, :] = (-(lanes[a] * keeps[a][48 * h:48 * h + 48])).astype(jnp.bfloat16)
 
@@ -259,15 +257,12 @@
         zz = lax.rem(z + jnp.where(t % 2 == 1, -s, s) + NZ, NZ)
         late(t, zz, yh).wait_send()
         core(t, zz).wait_send()
-
-        @pl.when(zz // 4 != x)
+        for d in (1, 2, 3):
+            xcopy(t, zz, d).wait_send()
+
+        @pl.when(jnp.logical_not(owned_here(zz)))
         def _():
-            xcopy(t, zz).wait_send()
-
-    for j in range(4):
-        ycopy(4 * x + j).wait_send()
-    for h in range(2):
-        fcopy(4 * x + 2 * (1 - k) + h).wait_send()
+            fcopy(t, zz).wait_send()
 
 
 def body(ainv, panel, structure, widths):
@@ -284,15 +279,13 @@
             pltpu.SMEM((4, 96), jnp.int32), pltpu.SMEM((4,), jnp.int32), vmem((6, 48, 256), bf16),
             vmem((3, 6, 256, 256), bf16),
             vmem((NZ, NY, 6, 48, 256), bf16),
-            vmem((NZ, 2, 2, 48, 384), f32),
-            vmem((NZ, 2, 48, 384), f32),
-            vmem((3, 4, 2, 48, 384), f32),
-            vmem((4, 48, 384), f32),
-            vmem((2, 48, 384), f32),
-            vmem((2, 48, 384), f32),
+            vmem((NZ, 2, 4, 24, 384), f32),
+            vmem((NZ, 4, 24, 384), f32),
+            vmem((NZ, 3, 24, 384), f32),
+            vmem((2, 2, 2, 2, 24, 384), f32),
             dma((4,)), dma, dma, dma((9, 3)), dma((9, 3)), dma((9, 3)), dma((9, 3)),
-            dma((16,)), dma((16,)), dma((16,)), dma((16,)), dma((16,)), dma((3, 4)),
-            dma((4,)), dma((4,)), dma((2,)), dma((2,)),
+            dma((16,)), dma((16,)), dma((16,)), dma((16,)), dma((16, 3)), dma((16, 3)),
+            dma((16,)), dma((2, 2, 2, 2)),
         ],
         compiler_params=pltpu.CompilerParams(
             collective_id=0, has_side_effects=True, vmem_limit_bytes=60 << 20),

time: 94.7 us -> 78.4 us (0.83)
  the two profiles are of different devices: /device:TPU:36 before, /device:TPU:11 now
where the time goes in v3:
time: 78.4 us; the launch traced here: 78.2 us
  Pallas kernels  76.7 us (98%)
  local copies, waits for them, and re-layouts  1.58 us (2%)
    pallas_call x1, Pallas kernels, body(): pl.pallas_call(kernel, out_shape=jax.ShapeDtypeStruct((3, 96, 256), bf16)...  76.7 us
    unnamed x1, local copies, waits for them, and re-layouts  1.58 us

profile of v3, /device:TPU:11, one launch (start us, length us, event | category | flops | bytes accessed | tf_op | source)
XLA Modules:
  0.0 78.2 jit_solution(11439642537659481408)
XLA Ops:
  0.0 76.7 %gather_multiply_scatter.1 = bf16[3,96,256]{2,1,0:T(8,128)(2,1)} custom-call(s32[4,96]{1,0:T(4,128)} %struct_hbm.1, s32[4]{0:T(128)} %widths_hbm.1, bf16[6,48,256]{2,1,0:T(8,128)(2,1)} %bitcast.13, bf16[3,6,256,256]{3,2,1,0:T(8,128)(2,1)} %bitcast.11), custom_call_target="tpu_custom_call" | custom-call | tf_op jit(solution)/shard_map/gather_multiply_scatter/pallas_call | solution.py:273
  76.7 1.6 %copy.7 = bf16[3,1,256,96]{2,3,1,0:T(8,128)(2,1)} copy(bf16[3,1,256,96]{2,3,1,0:T(8,128)(2,1)} %bitcast.12) | data formatting | bytes 294912

commit v4 on v3

--- a/solution.py
+++ b/solution.py
@@ -6,6 +6,7 @@
 from jax.sharding import PartitionSpec as P
 
 MESH = pl.DeviceIdType.MESH
+SUB = 1
 NZ, NY, NX, NK = 16, 2, 4, 2
 
 
@@ -46,7 +47,8 @@
         load.start()
     up_dev, dn_dev = dev(z=z_at(1)), dev(z=z_at(-1))
     pair_dev, core_dev = dev(yh=1 - yh), dev(k=1 - k)
-    partners = [up_dev, dn_dev, pair_dev] + [(row, lax.rem(col + d, npcol)) for d in range(1, npcol)]
+    over_dev, under_dev = dev(yh=1 - yh, z=z_at(1)), dev(yh=1 - yh, z=z_at(-1))
+    partners = [up_dev, dn_dev, pair_dev, over_dev, under_dev] + [(row, lax.rem(col + d, npcol)) for d in range(1, npcol)]
     barrier = pltpu.get_barrier_semaphore()
     for d in partners:
         pl.semaphore_signal(barrier, inc=1, device_id=d, device_id_type=MESH)
@@ -66,9 +68,10 @@
         return pbuf.at[zz, y, pl.ds(3 if second else 0, 3)]
 
     def ring(sems, device):
-        def message(s, h, zz):
-            ref = piece(zz, 1 - yh if h == 2 else yh, h > 0)
-            return remote(ref, ref, sems[0].at[s, h], sems[1].at[s, h], device)
+        def message(s, h, zz, i):
+            first, n = (3 if h > 0 else 0) + i * (3 // SUB), 3 // SUB
+            ref = pbuf.at[zz, 1 - yh if h == 2 else yh, pl.ds(first, n)]
+            return remote(ref, ref, sems[0].at[s, h, i], sems[1].at[s, h, i], device)
         return message
 
     up, dn = ring((up_s, up_r), up_dev), ring((dn_s, dn_r), dn_dev)
@@ -79,9 +82,12 @@
     def late(t, zz, y):
         return remote(piece(zz, y, False), piece(zz, y, False), late_s.at[t], late_r.at[t], pair_dev)
 
-    def products(zs):
+    def last_late():
+        return remote(piece(z_at(-7), yh, False), piece(z_at(-7), yh, False), late_s.at[15], late_r.at[15], over_dev)
+
+    def products(zs, which):
         n = len(zs)
-        for a in range(3):
+        for a in which:
             total = None
             for b in range(6):
                 rows = [pbuf[zz, :, b].reshape(96, 256) for zz in zs]
@@ -150,13 +156,6 @@
             def _(t=t, zz=zz):
                 stage(t, lax.rem(zz + NZ, NZ))
 
-    def multiply(s):
-        for t, zz in items(s):
-            late(t, zz, 1 - yh).wait_recv()
-        products([zz for _, zz in items(s)])
-        for t, zz in items(s):
-            core(t, zz).start()
-
     def when(s, do):
         if isinstance(s, int):
             if s < 7:
@@ -164,56 +163,68 @@
         else:
             pl.when(s < 7)(do)
 
+    def pass_both(s, h, up_on, dn_on):
+        below, above = z_at(-s), z_at(s)
+        for i in range(SUB):
+            up(s, h, below, i).wait_recv()
+            if up_on:
+                up(s + 1, h, below, i).start()
+            else:
+                when(s, up(s + 1, h, below, i).start)
+            dn(s, h, above, i).wait_recv()
+            if dn_on:
+                dn(s + 1, h, above, i).start()
+            else:
+                when(s, dn(s + 1, h, above, i).start)
+
+    def multiply(s):
+        for t, zz in items(s):
+            late(t, zz, 1 - yh).wait_recv()
+        products([zz for _, zz in items(s)], range(3))
+        for t, zz in items(s):
+            core(t, zz).start()
+
     def step(s):
-        last = isinstance(s, int) and s == 8
-        below, above = z_at(-s), z_at(s)
-        up(s, 0, below).wait_recv()
-        if not last:
-            up(s + 1, 0, below).start()
-            dn(s, 0, above).wait_recv()
-            when(s, dn(s + 1, 0, above).start)
+        pass_both(s, 0, True, False)
+        if not isinstance(s, int):
+            pl.when(s == 7)(last_late().start)
         for t, zz in items(s):
             late(t, zz, yh).start()
-        if not (isinstance(s, int) and s < 2):
-            multiply(s - 2)
-        if not last:
-            up(s, 1, below).wait_recv()
-            when(s, up(s + 1, 1, below).start)
-        dn(s, 1, above).wait_recv()
-        if not last:
-            dn(s + 1, 1, above).start()
-        run(stage_c, s - 3)
-        up(s, 2, below).wait_recv()
-        if not last:
-            up(s + 1, 2, below).start()
-            dn(s, 2, above).wait_recv()
-            when(s, dn(s + 1, 2, above).start)
-        run(stage_s, s - 5)
+        run(stage_c, s - 2)
+        pass_both(s, 1, False, True)
+        pass_both(s, 2, True, False)
+        multiply(s - 1)
+        run(stage_s, s - 3)
 
     for h in range(2):
-        up(1, h, z).start()
-        dn(1, h, z).start()
+        for i in range(SUB):
+            up(1, h, z, i).start()
+            dn(1, h, z, i).start()
         if h == 0:
             pair(yh).start()
     late(0, z, yh).start()
+    pair(1 - yh).wait_recv()
+    for i in range(SUB):
+        up(1, 2, z, i).start()
+        dn(1, 2, z, i).start()
     loads[3].wait()
-    pair(1 - yh).wait_recv()
-    up(1, 2, z).start()
-    dn(1, 2, z).start()
     step(1)
-    step(2)
-
-    @pl.loop(3, 8)
+
+    @pl.loop(2, 8)
     def _(s):
         step(s)
 
-    step(8)
+    for i in range(SUB):
+        up(8, 0, z_at(8), i).wait_recv()
+    run(stage_c, 6)
+    for i in range(SUB):
+        dn(8, 1, z_at(8), i).wait_recv()
+    for i in range(SUB):
+        up(8, 2, z_at(8), i).wait_recv()
     multiply(7)
-    run(stage_c, 6)
-    run(stage_s, 4)
+    run(stage_s, 5)
     multiply(8)
     run(stage_c, 7)
-    run(stage_s, 5)
     run(stage_c, 8)
     run(stage_s, 6)
     run(stage_s, 7)
@@ -244,18 +255,24 @@
     @pl.loop(1, 8)
     def _(s):
         for h in range(3):
-            up(s, h, z).wait_send()
-            dn(s, h, z).wait_send()
-
-    up(8, 0, z).wait_send()
-    up(8, 2, z).wait_send()
-    dn(8, 1, z).wait_send()
+            for i in range(SUB):
+                up(s, h, z, i).wait_send()
+                dn(s, h, z, i).wait_send()
+
+    @pl.loop(0, 15)
+    def _(t):
+        late(t, z, yh).wait_send()
+
+    last_late().wait_send()
+    for i in range(SUB):
+        up(8, 0, z, i).wait_send()
+        up(8, 2, z, i).wait_send()
+        dn(8, 1, z, i).wait_send()
 
     @pl.loop(0, 16)
     def _(t):
         s = (t + 1) // 2
         zz = lax.rem(z + jnp.where(t % 2 == 1, -s, s) + NZ, NZ)
-        late(t, zz, yh).wait_send()
         core(t, zz).wait_send()
         for d in (1, 2, 3):
             xcopy(t, zz, d).wait_send()
@@ -283,7 +300,7 @@
             vmem((NZ, 4, 24, 384), f32),
             vmem((NZ, 3, 24, 384), f32),
             vmem((2, 2, 2, 2, 24, 384), f32),
-            dma((4,)), dma, dma, dma((9, 3)), dma((9, 3)), dma((9, 3)), dma((9, 3)),
+            dma((4,)), dma, dma, dma((9, 3, SUB)), dma((9, 3, SUB)), dma((9, 3, SUB)), dma((9, 3, SUB)),
             dma((16,)), dma((16,)), dma((16,)), dma((16,)), dma((16, 3)), dma((16, 3)),
             dma((16,)), dma((2, 2, 2, 2)),
         ],

time: 78.4 us -> 74.9 us (0.955)
  Pallas kernels: 76.7 us -> 73.2 us
    pallas_call x1, Pallas kernels: 76.7 us -> 73.2 us  [body(): pl.pallas_call(kernel, out_shape=jax.ShapeDtypeStruct((3, 96, 256), bf16)...]
where the time goes in v4:
time: 74.9 us; the launch traced here: 74.8 us
  Pallas kernels  73.2 us (98%)
  local copies, waits for them, and re-layouts  1.58 us (2%)
    pallas_call x1, Pallas kernels, body(): pl.pallas_call(kernel, out_shape=jax.ShapeDtypeStruct((3, 96, 256), bf16)...  73.2 us
    unnamed x1, local copies, waits for them, and re-layouts  1.58 us

profile of v4, /device:TPU:11, one launch (start us, length us, event | category | flops | bytes accessed | tf_op | source)
XLA Modules:
  0.0 74.8 jit_solution(12444079200010923944)
XLA Ops:
  0.0 73.2 %gather_multiply_scatter.1 = bf16[3,96,256]{2,1,0:T(8,128)(2,1)} custom-call(s32[4,96]{1,0:T(4,128)} %struct_hbm.1, s32[4]{0:T(128)} %widths_hbm.1, bf16[6,48,256]{2,1,0:T(8,128)(2,1)} %bitcast.13, bf16[3,6,256,256]{3,2,1,0:T(8,128)(2,1)} %bitcast.11), custom_call_target="tpu_custom_call" | custom-call | tf_op jit(solution)/shard_map/gather_multiply_scatter/pallas_call | solution.py:290
  73.2 1.6 %copy.7 = bf16[3,1,256,96]{2,3,1,0:T(8,128)(2,1)} copy(bf16[3,1,256,96]{2,3,1,0:T(8,128)(2,1)} %bitcast.12) | data formatting | bytes 294912

commit v5 on v4

--- a/solution.py
+++ b/solution.py
@@ -6,7 +6,6 @@
 from jax.sharding import PartitionSpec as P
 
 MESH = pl.DeviceIdType.MESH
-SUB = 1
 NZ, NY, NX, NK = 16, 2, 4, 2
 
 
@@ -68,10 +67,9 @@
         return pbuf.at[zz, y, pl.ds(3 if second else 0, 3)]
 
     def ring(sems, device):
-        def message(s, h, zz, i):
-            first, n = (3 if h > 0 else 0) + i * (3 // SUB), 3 // SUB
-            ref = pbuf.at[zz, 1 - yh if h == 2 else yh, pl.ds(first, n)]
-            return remote(ref, ref, sems[0].at[s, h, i], sems[1].at[s, h, i], device)
+        def message(s, h, zz):
+            ref = piece(zz, 1 - yh if h == 2 else yh, h > 0)
+            return remote(ref, ref, sems[0].at[s, h], sems[1].at[s, h], device)
         return message
 
     up, dn = ring((up_s, up_r), up_dev), ring((dn_s, dn_r), dn_dev)
@@ -138,6 +136,10 @@
         def _():
             fcopy(t, zz).start()
 
+    def z_of(t):
+        s = (t + 1) // 2
+        return lax.rem(z + jnp.where(t % 2 == 1, -s, s) + NZ, NZ)
+
     def items(s):
         if isinstance(s, int):
             if s == 0:
@@ -165,23 +167,23 @@
 
     def pass_both(s, h, up_on, dn_on):
         below, above = z_at(-s), z_at(s)
-        for i in range(SUB):
-            up(s, h, below, i).wait_recv()
-            if up_on:
-                up(s + 1, h, below, i).start()
-            else:
-                when(s, up(s + 1, h, below, i).start)
-            dn(s, h, above, i).wait_recv()
-            if dn_on:
-                dn(s + 1, h, above, i).start()
-            else:
-                when(s, dn(s + 1, h, above, i).start)
-
-    def multiply(s):
-        for t, zz in items(s):
+        up(s, h, below).wait_recv()
+        if up_on:
+            up(s + 1, h, below).start()
+        else:
+            when(s, up(s + 1, h, below).start)
+        dn(s, h, above).wait_recv()
+        if dn_on:
+            dn(s + 1, h, above).start()
+        else:
+            when(s, dn(s + 1, h, above).start)
+
+    def multiply(*steps):
+        pairs = [item for s in steps for item in items(s)]
+        for t, zz in pairs:
             late(t, zz, 1 - yh).wait_recv()
-        products([zz for _, zz in items(s)], range(3))
-        for t, zz in items(s):
+        products([zz for _, zz in pairs], range(3))
+        for t, zz in pairs:
             core(t, zz).start()
 
     def step(s):
@@ -197,16 +199,14 @@
         run(stage_s, s - 3)
 
     for h in range(2):
-        for i in range(SUB):
-            up(1, h, z, i).start()
-            dn(1, h, z, i).start()
+        up(1, h, z).start()
+        dn(1, h, z).start()
         if h == 0:
             pair(yh).start()
     late(0, z, yh).start()
     pair(1 - yh).wait_recv()
-    for i in range(SUB):
-        up(1, 2, z, i).start()
-        dn(1, 2, z, i).start()
+    up(1, 2, z).start()
+    dn(1, 2, z).start()
     loads[3].wait()
     step(1)
 
@@ -214,21 +214,43 @@
     def _(s):
         step(s)
 
-    for i in range(SUB):
-        up(8, 0, z_at(8), i).wait_recv()
+    up(8, 0, z_at(8)).wait_recv()
     run(stage_c, 6)
-    for i in range(SUB):
-        dn(8, 1, z_at(8), i).wait_recv()
-    for i in range(SUB):
-        up(8, 2, z_at(8), i).wait_recv()
-    multiply(7)
+    dn(8, 1, z_at(8)).wait_recv()
+    up(8, 2, z_at(8)).wait_recv()
     run(stage_s, 5)
-    multiply(8)
+    multiply(7, 8)
     run(stage_c, 7)
     run(stage_c, 8)
     run(stage_s, 6)
+    pair(yh).wait_send()
+
+    @pl.loop(1, 8)
+    def _(s):
+        for h in range(3):
+            up(s, h, z).wait_send()
+            dn(s, h, z).wait_send()
+
+    @pl.loop(0, 15)
+    def _(t):
+        late(t, z, yh).wait_send()
+
+    last_late().wait_send()
+    up(8, 0, z).wait_send()
+    up(8, 2, z).wait_send()
+    dn(8, 1, z).wait_send()
+
+    @pl.loop(0, 16)
+    def _(t):
+        core(t, z_of(t)).wait_send()
+
     run(stage_s, 7)
     run(stage_s, 8)
+
+    @pl.loop(0, 16)
+    def _(t):
+        for d in (1, 2, 3):
+            xcopy(t, z_of(t), d).wait_send()
 
     masks = supernode_masks(widths_ref, col * 96, (96, 256))
     keeps = [keep_of(masks, struct_ref, a * nprow + row) for a in range(3)]
@@ -250,32 +272,9 @@
         for a in range(3):
             o_ref[a, 48 * h:48 * h + 48, :] = (-(lanes[a] * keeps[a][48 * h:48 * h + 48])).astype(jnp.bfloat16)
 
-    pair(yh).wait_send()
-
-    @pl.loop(1, 8)
-    def _(s):
-        for h in range(3):
-            for i in range(SUB):
-                up(s, h, z, i).wait_send()
-                dn(s, h, z, i).wait_send()
-
-    @pl.loop(0, 15)
-    def _(t):
-        late(t, z, yh).wait_send()
-
-    last_late().wait_send()
-    for i in range(SUB):
-        up(8, 0, z, i).wait_send()
-        up(8, 2, z, i).wait_send()
-        dn(8, 1, z, i).wait_send()
-
     @pl.loop(0, 16)
     def _(t):
-        s = (t + 1) // 2
-        zz = lax.rem(z + jnp.where(t % 2 == 1, -s, s) + NZ, NZ)
-        core(t, zz).wait_send()
-        for d in (1, 2, 3):
-            xcopy(t, zz, d).wait_send()
+        zz = z_of(t)
 
         @pl.when(jnp.logical_not(owned_here(zz)))
         def _():
@@ -290,7 +289,7 @@
     out = pl.pallas_call(
         kernel,
         out_shape=jax.ShapeDtypeStruct((3, 96, 256), bf16),
-        in_specs=[pl.BlockSpec(memory_space=pl.ANY)] * 4,
+        in_specs=[pl.BlockSpec(memory_space=pltpu.HBM)] * 4,
         out_specs=pl.BlockSpec(memory_space=vmem),
         scratch_shapes=[
             pltpu.SMEM((4, 96), jnp.int32), pltpu.SMEM((4,), jnp.int32), vmem((6, 48, 256), bf16),
@@ -300,14 +299,14 @@
             vmem((NZ, 4, 24, 384), f32),
             vmem((NZ, 3, 24, 384), f32),
             vmem((2, 2, 2, 2, 24, 384), f32),
-            dma((4,)), dma, dma, dma((9, 3, SUB)), dma((9, 3, SUB)), dma((9, 3, SUB)), dma((9, 3, SUB)),
+            dma((4,)), dma, dma, dma((9, 3)), dma((9, 3)), dma((9, 3)), dma((9, 3)),
             dma((16,)), dma((16,)), dma((16,)), dma((16,)), dma((16, 3)), dma((16, 3)),
             dma((16,)), dma((2, 2, 2, 2)),
         ],
         compiler_params=pltpu.CompilerParams(
-            collective_id=0, has_side_effects=True, vmem_limit_bytes=60 << 20),
+            collective_id=0, has_side_effects=True, vmem_limit_bytes=32 << 20),
         name="gather_multiply_scatter",
-    )(structure, widths, p, a)
+    )(*(pltpu.with_memory_space_constraint(v, pltpu.HBM) for v in (structure, widths, p, a)))
     return out.transpose(0, 2, 1)[:, None]
 
 

time: 74.9 us -> 72.4 us (0.967)
  Pallas kernels: 73.2 us -> 71.6 us
  local copies, waits for them, and re-layouts: 1.58 us -> 0.66 us
    pallas_call x1, Pallas kernels: 73.2 us -> 71.6 us  [body(): pl.pallas_call(kernel, out_shape=jax.ShapeDtypeStruct((3, 96, 256), bf16)...]
    unnamed x1, local copies, waits for them, and re-layouts: 1.58 us -> 0.66 us
where the time goes in v5:
time: 72.4 us; the launch traced here: 72.3 us
  Pallas kernels  71.6 us (99%)
    pallas_call x1, Pallas kernels, body(): pl.pallas_call(kernel, out_shape=jax.ShapeDtypeStruct((3, 96, 256), bf16)...  71.6 us

profile of v5, /device:TPU:11, one launch (start us, length us, event | category | flops | bytes accessed | tf_op | source)
XLA Modules:
  0.0 72.3 jit_solution(1412649151798051529)
XLA Ops:
  0.0 71.6 %gather_multiply_scatter.1 = bf16[3,96,256]{2,1,0:T(8,128)(2,1)S(1)} custom-call(s32[4,96]{1,0:T(4,128)} %struct_hbm.1, s32[4]{0:T(128)} %widths_hbm.1, bf16[6,48,256]{2,1,0:T(8,128)(2,1)} %bitcast.13, bf16[3,6,256,256]{3,2,1,0:T(8,128)(2,1)} %bitcast.12), custom_call_target="tpu_custom_call" | custom-call | tf_op jit(solution)/shard_map/gather_multiply_scatter/pallas_call | solution.py:289
  71.6 0.7 copy.7

commit v6 on v5

--- a/solution.py
+++ b/solution.py
@@ -27,7 +27,8 @@
 
 
 def kernel(struct_hbm, widths_hbm, p_hbm, a_hbm, o_ref, struct_ref, widths_ref, own, abuf, pbuf, part, crecv, xrecv, frecv,
-           in_sem, pair_s, pair_r, up_s, up_r, dn_s, dn_r, late_s, late_r, core_s, core_r, x_s, x_r, f_s, f_r):
+           in_sem, pair_s, pair_r, up_s, up_r, dn_s, dn_r, late_s, late_r, core_s, core_r, x_s, x_r, f_s, f_r,
+           known):
     row = lax.axis_index("prow")
     col = lax.axis_index("pcol")
     nprow, npcol = lax.axis_size("prow"), lax.axis_size("pcol")
@@ -45,9 +46,18 @@
     for load in loads:
         load.start()
     up_dev, dn_dev = dev(z=z_at(1)), dev(z=z_at(-1))
-    pair_dev, core_dev = dev(yh=1 - yh), dev(k=1 - k)
-    over_dev, under_dev = dev(yh=1 - yh, z=z_at(1)), dev(yh=1 - yh, z=z_at(-1))
-    partners = [up_dev, dn_dev, pair_dev, over_dev, under_dev] + [(row, lax.rem(col + d, npcol)) for d in range(1, npcol)]
+    pair_dev, core_dev, over_dev = dev(yh=1 - yh), dev(k=1 - k), dev(yh=1 - yh, z=z_at(1))
+    y_dev, next_dev = dev(yl=1 - yl), dev(x=lax.rem(x + 1, NX))
+    partners = [up_dev, dn_dev, pair_dev, core_dev, y_dev, next_dev, dev(x=lax.rem(x + 3, NX))]
+    rounds = [[core_dev, pair_dev], [y_dev], [next_dev]]
+
+    def tell(i):
+        for d in rounds[i]:
+            pl.semaphore_signal(known.at[i], inc=1, device_id=d, device_id_type=MESH)
+
+    def learn(i):
+        pl.semaphore_wait(known.at[i], len(rounds[i]))
+
     barrier = pltpu.get_barrier_semaphore()
     for d in partners:
         pl.semaphore_signal(barrier, inc=1, device_id=d, device_id_type=MESH)
@@ -204,11 +214,17 @@
         if h == 0:
             pair(yh).start()
     late(0, z, yh).start()
+    tell(0)
     pair(1 - yh).wait_recv()
     up(1, 2, z).start()
     dn(1, 2, z).start()
     loads[3].wait()
+    learn(0)
+    tell(1)
+    learn(1)
+    tell(2)
     step(1)
+    learn(2)
 
     @pl.loop(2, 8)
     def _(s):
@@ -301,7 +317,7 @@
             vmem((2, 2, 2, 2, 24, 384), f32),
             dma((4,)), dma, dma, dma((9, 3)), dma((9, 3)), dma((9, 3)), dma((9, 3)),
             dma((16,)), dma((16,)), dma((16,)), dma((16,)), dma((16, 3)), dma((16, 3)),
-            dma((16,)), dma((2, 2, 2, 2)),
+            dma((16,)), dma((2, 2, 2, 2)), pltpu.SemaphoreType.REGULAR((3,)),
         ],
         compiler_params=pltpu.CompilerParams(
             collective_id=0, has_side_effects=True, vmem_limit_bytes=32 << 20),

time: 72.4 us -> 71.5 us (0.988)
  Pallas kernels: 71.6 us -> 70.7 us
    pallas_call x1, Pallas kernels: 71.6 us -> 70.7 us  [body(): pl.pallas_call(kernel, out_shape=jax.ShapeDtypeStruct((3, 96, 256), bf16)...]
where the time goes in v6:
time: 71.5 us; the launch traced here: 71.4 us
  Pallas kernels  70.7 us (99%)
    pallas_call x1, Pallas kernels, body(): pl.pallas_call(kernel, out_shape=jax.ShapeDtypeStruct((3, 96, 256), bf16)...  70.7 us

profile of v6, /device:TPU:11, one launch (start us, length us, event | category | flops | bytes accessed | tf_op | source)
XLA Modules:
  0.0 71.4 jit_solution(7662050573545708220)
XLA Ops:
  0.0 70.7 %gather_multiply_scatter.1 = bf16[3,96,256]{2,1,0:T(8,128)(2,1)S(1)} custom-call(s32[4,96]{1,0:T(4,128)} %struct_hbm.1, s32[4]{0:T(128)} %widths_hbm.1, bf16[6,48,256]{2,1,0:T(8,128)(2,1)} %bitcast.13, bf16[3,6,256,256]{3,2,1,0:T(8,128)(2,1)} %bitcast.12), custom_call_target="tpu_custom_call" | custom-call | tf_op jit(solution)/shard_map/gather_multiply_scatter/pallas_call | solution.py:305
  70.7 0.7 copy.7

commit v7 on v6

--- a/solution.py
+++ b/solution.py
@@ -46,7 +46,7 @@
     for load in loads:
         load.start()
     up_dev, dn_dev = dev(z=z_at(1)), dev(z=z_at(-1))
-    pair_dev, core_dev, over_dev = dev(yh=1 - yh), dev(k=1 - k), dev(yh=1 - yh, z=z_at(1))
+    pair_dev, core_dev, under_dev = dev(yh=1 - yh), dev(k=1 - k), dev(yh=1 - yh, z=z_at(-1))
     y_dev, next_dev = dev(yl=1 - yl), dev(x=lax.rem(x + 1, NX))
     partners = [up_dev, dn_dev, pair_dev, core_dev, y_dev, next_dev, dev(x=lax.rem(x + 3, NX))]
     rounds = [[core_dev, pair_dev], [y_dev], [next_dev]]
@@ -91,7 +91,7 @@
         return remote(piece(zz, y, False), piece(zz, y, False), late_s.at[t], late_r.at[t], pair_dev)
 
     def last_late():
-        return remote(piece(z_at(-7), yh, False), piece(z_at(-7), yh, False), late_s.at[15], late_r.at[15], over_dev)
+        return remote(piece(z_at(7), yh, False), piece(z_at(7), yh, False), late_s.at[15], late_r.at[15], under_dev)
 
     def products(zs, which):
         n = len(zs)
@@ -115,17 +115,22 @@
     def core(t, zz):
         return remote(part.at[zz, 1 - k], crecv.at[zz], core_s.at[t], core_r.at[t], core_dev)
 
+    def quarter(x):
+        return x % 2 * 2 + x // 2
+
+    mine = quarter(x)
+
     def xcopy(t, zz, d):
         to = lax.rem(x + d, NX)
-        return remote(part.at[zz, k, to], xrecv.at[zz, d - 1], x_s.at[t, d - 1], x_r.at[t, d - 1], dev(x=to))
+        return remote(part.at[zz, k, quarter(to)], xrecv.at[zz, d - 1], x_s.at[t, d - 1], x_r.at[t, d - 1], dev(x=to))
 
     def owned_here(zz):
-        return (zz // 4 == x) & (x // 2 == yl) & ((zz // 2) % 2 == k)
+        return (zz // 4 == x) & (x % 2 == yl) & ((zz // 2) % 2 == k)
 
     def fcopy(t, zz):
-        h, rh = zz % 2, x % 2
-        return remote(part.at[zz, k, x], frecv.at[h, rh, yl, k], f_s.at[t], f_r.at[h, rh, yl, k],
-                      dev(x=zz // 4, yl=x // 2, k=(zz // 2) % 2))
+        h, rh = zz % 2, x // 2
+        return remote(part.at[zz, k, mine], frecv.at[h, rh, yl, k], f_s.at[t], f_r.at[h, rh, yl, k],
+                      dev(x=zz // 4, yl=x % 2, k=(zz // 2) % 2))
 
     def stage_c(t, zz):
         core(t, zz).wait_recv()
@@ -136,11 +141,11 @@
     def stage_s(t, zz):
         for d in (2, 1, 3):
             xcopy(t, zz, d).wait_recv()
-        part[zz, k, x] = part[zz, k, x] + xrecv[zz, 0] + xrecv[zz, 1] + xrecv[zz, 2]
+        part[zz, k, mine] = part[zz, k, mine] + xrecv[zz, 0] + xrecv[zz, 1] + xrecv[zz, 2]
 
         @pl.when(owned_here(zz))
         def _():
-            frecv[zz % 2, x % 2, yl, k] = part[zz, k, x]
+            frecv[zz % 2, x // 2, yl, k] = part[zz, k, mine]
 
         @pl.when(jnp.logical_not(owned_here(zz)))
         def _():
@@ -276,7 +281,7 @@
         for rh in range(2):
             for ys in range(2):
                 for ks in range(2):
-                    here = (x == 2 * yl + rh) & (ys == yl) & (ks == k)
+                    here = (x == 2 * rh + yl) & (ys == yl) & (ks == k)
 
                     @pl.when(jnp.logical_not(here))
                     def _(rh=rh, ys=ys, ks=ks):

time: 71.5 us -> 71.5 us (level)
  no operation moved by 1% of the time
where the time goes in v7:
time: 71.5 us; the launch traced here: 71.4 us
  Pallas kernels  70.7 us (99%)
    pallas_call x1, Pallas kernels, body(): pl.pallas_call(kernel, out_shape=jax.ShapeDtypeStruct((3, 96, 256), bf16)...  70.7 us

profile of v7, /device:TPU:11, one launch (start us, length us, event | category | flops | bytes accessed | tf_op | source)
XLA Modules:
  0.0 71.4 jit_solution(14993520826742957732)
XLA Ops:
  0.0 70.7 %gather_multiply_scatter.1 = bf16[3,96,256]{2,1,0:T(8,128)(2,1)S(1)} custom-call(s32[4,96]{1,0:T(4,128)} %struct_hbm.1, s32[4]{0:T(128)} %widths_hbm.1, bf16[6,48,256]{2,1,0:T(8,128)(2,1)} %bitcast.13, bf16[3,6,256,256]{3,2,1,0:T(8,128)(2,1)} %bitcast.12), custom_call_target="tpu_custom_call" | custom-call | tf_op jit(solution)/shard_map/gather_multiply_scatter/pallas_call | solution.py:310
  70.7 0.7 copy.7
